TPU v7x, 32 devices: a whole 2x2x4 slice. The times are simulated.
32 devices in a mesh: row: 16 (over z, x, core), col: 2 (over y).
Axes of the slice: x: 2, y: 2, z: 4, core: 2. Of those that a mesh axis runs over, the one named last changes fastest.
Arguments:
- qkv: bfloat16 [256, 16, 3, 3072], P('row', 'col'), may hold values from -6 to 6
- cotangent: bfloat16 [256, 16, 3072], P('row', 'col'), may hold values from -6 to 6
- norm_gains: float32 [2, 128], replicated, may hold values from 0.1 to 1.9
- rel_table: float32 [24, 15, 15], replicated, may hold values from -6 to 250
- shifts: int32 [2], replicated, may hold values from 1 to 7
- mask_ids: int32 [256, 16], replicated, may hold values from 0 to 2
Outputs:
- attention: bfloat16 [256, 16, 3072], P('row', 'col')
- d_qkv: bfloat16 [256, 16, 3, 3072], P('row', 'col')
- d_gains: float32 [2, 128], replicated
- d_table: float32 [24, 15, 15], replicated
All inputs are finite; a program needn't handle non-finite values.
Results may differ from a plain program's by a relative error of at most 0.0073.
Values may be sent and summed in bfloat16 or wider, within the bound.
A program may use at most 192 MiB of HBM per device.

v0:
```python
import math
import jax
import jax.numpy as jnp
from jax import lax
from jax.sharding import PartitionSpec as P

EPSILON = 1e-06
NEG_FILL = -1e30


def shifted(value, axis, steps):
    count = lax.axis_size(axis)
    pairs = [(source, (source + steps) % count) for source in range(count)]
    return lax.ppermute(value, axis, pairs)


def head_norm(inputs, gain_vec):
    values = inputs.astype(jnp.float32)
    average = jnp.mean(values, axis=-1, keepdims=True)
    centred = values - average
    variance = jnp.mean(centred * centred, axis=-1, keepdims=True)
    inv_sigma = lax.rsqrt(variance + EPSILON)
    x_hat = centred * inv_sigma
    return (x_hat, inv_sigma, (x_hat * gain_vec).astype(jnp.bfloat16))


def norm_back(x_hat, inv_sigma, d_normed, gain_vec):
    d_hat = d_normed * gain_vec
    first_mean = jnp.mean(d_hat, axis=-1, keepdims=True)
    second_mean = jnp.mean(d_hat * x_hat, axis=-1, keepdims=True)
    d_input = inv_sigma * (d_hat - first_mean - x_hat * second_mean)
    d_gain = jnp.sum(d_normed * x_hat, axis=tuple(range(d_normed.ndim - 1)))
    return (d_input, d_gain)


def offset_table(window_size):
    span_count = 2 * window_size - 1
    places = jnp.arange(window_size * window_size, dtype=jnp.int32)
    row_pos = places // window_size
    col_pos = places % window_size
    code_grid = (row_pos[:, None] - row_pos[None, :] + window_size - 1) * span_count + (
        col_pos[:, None] - col_pos[None, :] + window_size - 1
    )
    codes = jnp.arange(span_count * span_count, dtype=jnp.int32)
    return (code_grid[:, :, None] == codes[None, None, :]).astype(jnp.float32)


def to_windows(field, window_size):
    row_count, col_count = (field.shape[0], field.shape[1])
    trailing = field.shape[2:]
    blocks = field.reshape(
        (row_count // window_size, window_size, col_count // window_size, window_size) + trailing
    )
    blocks = jnp.moveaxis(blocks, 2, 1)
    return blocks.reshape(
        (row_count // window_size * (col_count // window_size), window_size * window_size)
        + trailing
    )


def from_windows(blocks, window_size, row_count, col_count):
    trailing = blocks.shape[2:]
    field = blocks.reshape(
        (row_count // window_size, col_count // window_size, window_size, window_size) + trailing
    )
    field = jnp.moveaxis(field, 1, 2)
    return field.reshape((row_count, col_count) + trailing)


def window_core(q_norm, k_norm, values, grads, pos_bias, allowed, score_scale):
    scores = (
        jnp.einsum("wqhd,wkhd->whqk", q_norm, k_norm, preferred_element_type=jnp.float32)
        * score_scale
        + pos_bias[None]
    )
    scores = jnp.where(allowed[:, None], scores, NEG_FILL)
    row_max = jnp.max(scores, axis=-1, keepdims=True)
    weights = jnp.exp(scores - row_max)
    probs = weights / jnp.sum(weights, axis=-1, keepdims=True)
    probs_b = probs.astype(jnp.bfloat16)
    output = jnp.einsum("whqk,wkhd->wqhd", probs_b, values, preferred_element_type=jnp.float32)
    d_probs = jnp.einsum("wqhd,wkhd->whqk", grads, values, preferred_element_type=jnp.float32)
    row_dot = jnp.sum(probs * d_probs, axis=-1, keepdims=True)
    d_scores = probs * (d_probs - row_dot)
    d_scores_b = d_scores.astype(jnp.bfloat16)
    d_qnorm = (
        jnp.einsum("whqk,wkhd->wqhd", d_scores_b, k_norm, preferred_element_type=jnp.float32)
        * score_scale
    )
    d_knorm = (
        jnp.einsum("whqk,wqhd->wkhd", d_scores_b, q_norm, preferred_element_type=jnp.float32)
        * score_scale
    )
    d_value = jnp.einsum("whqk,wqhd->wkhd", probs_b, grads, preferred_element_type=jnp.float32)
    return (output, d_qnorm, d_knorm, d_value, jnp.sum(d_scores, axis=0))


def label_pairs(labels, window_size):
    label_win = to_windows(labels, window_size)
    return label_win[:, :, None] == label_win[:, None, :]


def local(qkv, cotangent, norm_gains, rel_table, shifts, mask_ids):
    tile_rows, tile_cols = (qkv.shape[0], qkv.shape[1])
    feature_width = qkv.shape[3]
    head_count = rel_table.shape[0]
    head_dim = feature_width // head_count
    span_count = rel_table.shape[1]
    window_size = (span_count + 1) // 2
    score_scale = 1.0 / math.sqrt(head_dim)
    shift_row = shifts[0]
    shift_col = shifts[1]
    grid_row = lax.axis_index("row") * tile_rows
    grid_col = lax.axis_index("col") * tile_cols
    one_hot = offset_table(window_size)
    pos_bias = jnp.einsum(
        "hc,qkc->hqk",
        rel_table.reshape(head_count, span_count * span_count),
        one_hot,
        precision=lax.Precision.HIGHEST,
    )
    gain_q = norm_gains[0]
    gain_k = norm_gains[1]
    stacked = jnp.concatenate([qkv, cotangent[:, :, None]], axis=2)
    received = shifted(stacked[:window_size], "row", -1)
    rolled = lax.dynamic_slice_in_dim(
        jnp.concatenate([stacked, received], axis=0), shift_row, tile_rows, 0
    )
    received = shifted(rolled, "col", -1)
    rolled = lax.dynamic_slice_in_dim(
        jnp.concatenate([rolled, received], axis=1), shift_col, tile_cols, 1
    )
    fields = rolled.reshape(tile_rows, tile_cols, 4, head_count, head_dim)
    q_hat, q_inv, q_norm = head_norm(fields[:, :, 0], gain_q)
    k_hat, k_inv, k_norm = head_norm(fields[:, :, 1], gain_k)
    labels = jnp.roll(mask_ids, (-(grid_row + shift_row), -(grid_col + shift_col)), (0, 1))[
        :tile_rows, :tile_cols
    ]
    output, d_qnorm, d_knorm, d_value, d_bias = window_core(
        to_windows(q_norm, window_size),
        to_windows(k_norm, window_size),
        to_windows(fields[:, :, 2], window_size),
        to_windows(fields[:, :, 3], window_size),
        pos_bias,
        label_pairs(labels, window_size),
        score_scale,
    )
    output = from_windows(output, window_size, tile_rows, tile_cols)
    d_qnorm = from_windows(d_qnorm, window_size, tile_rows, tile_cols)
    d_knorm = from_windows(d_knorm, window_size, tile_rows, tile_cols)
    d_value = from_windows(d_value, window_size, tile_rows, tile_cols)
    d_query, dgain_q = norm_back(q_hat, q_inv, d_qnorm, gain_q)
    d_key, dgain_k = norm_back(k_hat, k_inv, d_knorm, gain_k)
    results = (
        jnp.stack([output, d_query, d_key, d_value], axis=2)
        .reshape(tile_rows, tile_cols, 4, feature_width)
        .astype(jnp.bfloat16)
    )
    received = shifted(results[tile_rows - window_size :], "row", 1)
    results = lax.dynamic_slice_in_dim(
        jnp.concatenate([received, results], axis=0), window_size - shift_row, tile_rows, 0
    )
    received = shifted(results, "col", 1)
    results = lax.dynamic_slice_in_dim(
        jnp.concatenate([received, results], axis=1), window_size - shift_col, tile_cols, 1
    )
    attention = results[:, :, 0]
    d_qkv = results[:, :, 1:]
    table_local = jnp.einsum("hqk,qkc->hc", d_bias, one_hot, precision=lax.Precision.HIGHEST)
    totals = lax.psum((jnp.stack([dgain_q, dgain_k]), table_local), ("row", "col"))
    return (attention, d_qkv, totals[0], totals[1].reshape(head_count, span_count, span_count))


def solution(mesh):
    placed = (P("row", "col", None, None), P("row", "col", None), P(), P(), P(), P())
    return jax.shard_map(
        local,
        mesh=mesh,
        in_specs=placed,
        out_specs=(P("row", "col", None), P("row", "col", None, None), P(), P()),
        check_vma=False,
    )
```

profile of v0, /device:TPU:0, one launch (start us, length us, event | category | flops | bytes accessed | tf_op | source)
XLA Modules:
  0.0 298.4 jit_solution(15147776239652918049)
XLA Ops:
  0.6 1.5 pad_maximum_fusion
  2.2 5.5 %collective-permute-start = (bf16[8,8,4,3072]{3,1,2,0:T(8,128)(2,1)S(1)}, bf16[8,8,4,3072]{3,1,2,0:T(8,128)(2,1)}, u32[]{:S(2)}, u32[]{:S(2)}) collective-permute-start(bf16[8,8,4,3072]{3,1,2,0:T(8,128)(2,1)S(1)} %pad_maximum_fusion), channel_id=1, source_target_pairs={{0,30},{2,0},{4,2},{6,4},{8,6},{10,8},{12,10},{14,12},{16,14},{18,... | collective-permute-start | bytes 4718600 | tf_op jit(solution)/shard_map/ppermute | solution.py:14
  7.7 0.6 fusion.39
  10.2 15.4 %collective-permute-done = bf16[8,8,4,3072]{3,1,2,0:T(8,128)(2,1)} collective-permute-done((bf16[8,8,4,3072]{3,1,2,0:T(8,128)(2,1)S(1)}, bf16[8,8,4,3072]{3,1,2,0:T(8,128)(2,1)}, u32[]{:S(2)}, u32[]{:S(2)}) %collective-permute-start) | collective-permute-done | bytes 1572896 | tf_op jit(solution)/shard_map/ppermute | solution.py:14
  25.6 2.9 fusion.5
  28.5 1.6 collective-permute-start.1
  32.5 0.1 fusion.34
  32.6 0.1 copy.44
  32.7 0.1 eq.45
  32.8 0.1 add_add_fusion
  32.9 0.6 copy-done.11
  33.5 0.9 iota_compare_fusion
  34.4 4.5 %fusion.20 = f32[24,64,64]{2,0,1:T(8,128)} fusion(pred[64,64,225]{2,0,1:T(32,128)(4,1)S(1)} %iota_compare_fusion, f32[24,225]{0,1:T(8,128)S(1)} %reshape.290), kind=kOutput, calls=%fused_computation.52 | convolution fusion | flops 265420800 | bytes 1336416 | tf_op jit(solution)/shard_map/hc,qkc->hqk/dot_general | solution.py:116
  38.9 2.3 copy.53
  41.8 0.6 broadcast_multiply_fusion.6
  42.4 0.7 broadcast_compare_fusion
  43.1 53.5 %collective-permute-done.1 = bf16[16,8,4,3072]{3,1,2,0:T(8,128)(2,1)} collective-permute-done((bf16[16,8,4,3072]{3,1,2,0:T(8,128)(2,1)S(1)}, bf16[16,8,4,3072]{3,1,2,0:T(8,128)(2,1)}, u32[]{:S(2)}, u32[]{:S(2)}) %collective-permute-start.1) | collective-permute-done | bytes 3145760 | tf_op jit(solution)/shard_map/ppermute | solution.py:14
  96.6 4.0 %fusion.7 = bf16[16,8,4,3072]{3,1,2,0:T(8,128)(2,1)S(1)} fusion(s32[]{:T(128)S(6)} %select_n.71, bf16[16,8,4,3072]{3,1,2,0:T(8,128)(2,1)S(1)} %fusion.5, bf16[16,8,4,3072]{3,1,2,0:T(8,128)(2,1)} %collective-permute-done.1), kind=kLoop, calls=%fused_computation.17 | loop fusion | flops 6291456 | bytes 9437188 | tf_op jit(solution)/shard_map/concatenate | solution.py:131
  100.6 0.9 copy.76
  101.5 0.9 convert_reduce_fusion
  102.4 2.4 fusion.38
  104.8 1.9 fusion.12
  107.0 4.2 %add_select_fusion = f32[2,24,64,64]{2,3,1,0:T(8,128)S(1)} fusion(f32[24,64,64]{1,2,0:T(8,128)} %copy.53, pred[2,64,64]{1,2,0:T(8,128)(4,1)} %broadcast_compare_fusion, f32[2,64,24,128]{3,2,1,0:T(8,128)} %bitcast.113, f32[128]{0:T(128)S(1)} %get-tuple-element.35, f32[2,64,24]{1,2,0:T(8,128)S(1)} %copy.47, f32[2,64,24]{1,2,0:T(8,128)S(1)} %copy.45, ...), kind=kOutput, calls=%fused_computation.44 | convolution fusion | flops 54067200 | bytes 4383744 | tf_op jit(solution)/shard_map/wqhd,wkhd->whqk/dot_general | solution.py:72
  111.2 1.6 fusion.40
  112.9 3.6 %fusion.19 = bf16[2,64,24,128]{3,1,2,0:T(8,128)(2,1)} fusion(bf16[2,64,24,128]{3,2,1,0:T(8,128)(2,1)} %bitcast.120, f32[2,24,64]{2,1,0:T(8,128)S(1)} %get-tuple-element.38, f32[2,24,64,64]{2,3,1,0:T(8,128)} %copy-done.2), kind=kOutput, calls=%fused_computation.51 | convolution fusion | flops 51317824 | bytes 2371584 | tf_op jit(solution)/shard_map/whqk,wqhd->wkhd/dot_general | solution.py:94
  116.5 3.6 %fusion.18 = bf16[2,64,24,128]{3,1,2,0:T(8,128)(2,1)} fusion(bf16[2,64,24,128]{3,2,1,0:T(8,128)(2,1)} %bitcast.122, f32[2,24,64]{2,1,0:T(8,128)S(1)} %get-tuple-element.38, f32[2,24,64,64]{2,3,1,0:T(8,128)} %copy-done.2), kind=kOutput, calls=%fused_computation.50 | convolution fusion | flops 51317824 | bytes 2371584 | tf_op jit(solution)/shard_map/whqk,wkhd->wqhd/dot_general | solution.py:81
  120.1 2.5 copy.56
  122.6 2.2 stack.22
  124.8 2.5 copy.69
  127.3 2.2 stack.25
  129.5 2.6 multiply_reduce_fusion.2
  132.1 1.4 fusion.29
  133.5 0.7 copy-done.4
  134.2 4.8 %multiply_reduce_fusion = (f32[128]{0:T(128)}, f32[2,64,24]{1,2,0:T(8,128)S(1)}, f32[2,64,24]{1,2,0:T(8,128)S(1)}, f32[2,24,128,64]{2,3,1,0:T(8,128)}) fusion(f32[2,64,24,128]{3,2,1,0:T(8,128)S(1)} %bitcast.111, f32[2,64,24]{1,2,0:T(8,128)S(1)} %copy.50, f32[2,64,24]{1,2,0:T(8,128)S(1)} %copy.48, f32[128]{0:T(128)S(1)} %copy-done.20, ...), kind=kOutput, calls=%fused_computation.36 | convolution fusion | flops 55437184 | bytes 5187072 | tf_op jit(solution)/shard_map/whqk,wqhd->wkhd/dot_general | solution.py:91
  139.0 5.3 %multiply_reduce_fusion.1 = (f32[128]{0:T(128)}, f32[2,64,24]{1,2,0:T(8,128)S(1)}, f32[2,64,24]{1,2,0:T(8,128)S(1)}, f32[2,24,128,64]{2,3,1,0:T(8,128)}) fusion(f32[2,64,24,128]{3,2,1,0:T(8,128)S(1)} %bitcast.115, f32[2,64,24]{1,2,0:T(8,128)S(1)} %copy.47, f32[2,64,24]{1,2,0:T(8,128)S(1)} %copy.45, f32[128]{0:T(128)S(1)} %copy-done.19, ...), kind=kOutput, calls=%fused_computation.37 | convolution fusion | flops 55437184 | bytes 5187072 | tf_op jit(solution)/shard_map/whqk,wkhd->wqhd/dot_general | solution.py:87
  144.3 0.6 broadcast_multiply_fusion.2
  144.9 0.6 broadcast_multiply_fusion.3
  145.5 0.6 broadcast_multiply_fusion.4
  146.2 0.1 copy.62
  146.2 0.8 copy.63
  147.1 1.4 copy.66
  148.5 1.4 copy.67
  149.9 1.6 multiply_bitcast_fusion
  151.5 0.9 copy.64
  152.4 0.5 copy-done.8
  152.9 0.2 multiply_bitcast_fusion.1
  153.2 0.9 copy.60
  154.1 5.1 %multiply_convert_fusion = (bf16[16,8,1,24,128]{4,3,1,2,0:T(8,128)(2,1)}, bf16[16,8,1,24,128]{4,3,1,2,0:T(8,128)(2,1)}) fusion(f32[16,8,1,24,128]{4,3,1,2,0:T(8,128)S(1)} %bitcast.108, f32[16,8,24]{2,1,0:T(8,128)S(1)} %bitcast.129, f32[16,8,24]{2,1,0:T(8,128)S(1)} %get-tuple-element.46, f32[16,8,24]{2,1,0:T(8,128)S(1)} %bitcast.128, ...), kind=kLoop, calls=%fused_computation.38 | loop fusion | flops 7077888 | bytes 6390784 | tf_op jit(solution)/shard_map/convert.8
  159.2 1.5 stack.24
  160.8 0.3 stack.23
  161.3 1.0 copy-done.5
  162.4 0.1 slice.56
  162.5 1.5 copy-done
  165.4 21.3 %collective-permute-done.2 = bf16[8,8,4,3072]{3,1,0,2:T(8,128)(2,1)} collective-permute-done((bf16[8,8,4,3072]{3,1,0,2:T(8,128)(2,1)S(1)}, bf16[8,8,4,3072]{3,1,0,2:T(8,128)(2,1)}, u32[]{:S(2)}, u32[]{:S(2)}) %collective-permute-start.2) | collective-permute-done | bytes 1572896 | tf_op jit(solution)/shard_map/ppermute | solution.py:14
  186.7 2.6 fusion.3
  189.3 1.6 collective-permute-start.3
  192.1 2.8 convolution_bitcast_fusion
  194.9 0.1 reshape.285
  195.0 95.8 %all-reduce = (f32[2,128]{1,0:T(2,128)}, f32[24,15,15]{2,1,0:T(8,128)S(1)}) all-reduce(f32[2,128]{1,0:T(2,128)S(1)} %pad_maximum_fusion.1, f32[24,15,15]{2,1,0:T(8,128)S(1)} %reshape.285), channel_id=1, replica_groups=mesh['row'=16,'col'=2] {'row','col'}, use_global_device_ids=true, to_apply=%region_13.14 | all-reduce | flops 5656 | bytes 45248 | tf_op jit(solution)/shard_map/psum | solution.py:170
  290.9 0.8 copy.72
  291.7 4.0 %fusion.6 = bf16[16,8,4,3072]{3,1,0,2:T(8,128)(2,1)S(1)} fusion(s32[]{:T(128)S(6)} %select_n.80, bf16[16,8,4,3072]{3,1,0,2:T(8,128)(2,1)} %collective-permute-done.3, bf16[16,8,4,3072]{3,1,0,2:T(8,128)(2,1)S(1)} %fusion.3), kind=kLoop, calls=%fused_computation.16 | loop fusion | flops 6291456 | bytes 9437188 | tf_op jit(solution)/shard_map/concatenate | solution.py:165
  295.8 0.9 slice_bitcast_fusion
  296.7 0.2 slice.58
  296.8 1.6 copy.71
  (56 shorter events, 0.7 us)
Async XLA Ops:
  0.6 7.1 %copy-start.16 = (s32[2]{0:T(128)S(1)}, s32[2]{0:T(128)}, u32[]{:S(2)}) copy-start(s32[2]{0:T(128)} %param.10) | copy-start | bytes 28
  2.2 23.4 %collective-permute-start = (bf16[8,8,4,3072]{3,1,2,0:T(8,128)(2,1)S(1)}, bf16[8,8,4,3072]{3,1,2,0:T(8,128)(2,1)}, u32[]{:S(2)}, u32[]{:S(2)}) collective-permute-start(bf16[8,8,4,3072]{3,1,2,0:T(8,128)(2,1)S(1)} %pad_maximum_fusion), channel_id=1, source_target_pairs={{0,30},{2,0},{4,2},{6,4},{8,6},{10,8},{12,10},{14,12},{16,14},{18,... | collective-permute-start | bytes 4718600 | tf_op jit(solution)/shard_map/ppermute | solution.py:14
  10.2 22.3 %copy-start.14 = (s32[256,16]{0,1:T(8,128)S(1)}, s32[256,16]{0,1:T(8,128)}, u32[]{:S(2)}) copy-start(s32[256,16]{0,1:T(8,128)} %param.11) | copy-start | bytes 49156
  10.2 22.5 %copy-start.13 = (f32[24,15,15]{0,2,1:T(8,128)S(1)}, f32[24,15,15]{0,2,1:T(8,128)}, u32[]{:S(2)}) copy-start(f32[24,15,15]{0,2,1:T(8,128)} %param.9) | copy-start | bytes 64804
  28.5 68.1 %collective-permute-start.1 = (bf16[16,8,4,3072]{3,1,2,0:T(8,128)(2,1)S(1)}, bf16[16,8,4,3072]{3,1,2,0:T(8,128)(2,1)}, u32[]{:S(2)}, u32[]{:S(2)}) collective-permute-start(bf16[16,8,4,3072]{3,1,2,0:T(8,128)(2,1)S(1)} %fusion.5), channel_id=1, source_target_pairs={{0,1},{1,0},{2,3},{3,2},{4,5},{5,4},{6,7},{7,6},{8,9},{9,8},{10,11... | collective-permute-start | bytes 9437192 | tf_op jit(solution)/shard_map/ppermute | solution.py:14
  32.9 0.6 copy-start.11
  38.9 2.9 copy-start.15
  111.2 1.7 copy-start.2
  129.5 2.6 copy-start.1
  132.1 1.4 copy-start.3
  132.1 2.2 copy-start.4
  132.1 2.1 copy-start.20
  134.2 4.8 %copy-start.19 = (f32[128]{0:T(128)S(1)}, f32[128]{0:T(128)}, u32[]{:S(2)}) copy-start(f32[128]{0:T(128)} %get-tuple-element.33) | copy-start | bytes 1540
  151.5 1.4 copy-start.8
  153.2 0.9 copy-start.9
  153.2 0.9 copy-start.10
  159.2 1.6 copy-start.7
  159.2 1.9 copy-start.6
  161.2 1.1 copy-start.5
  162.4 1.7 copy-start
  164.1 22.6 %collective-permute-start.2 = (bf16[8,8,4,3072]{3,1,0,2:T(8,128)(2,1)S(1)}, bf16[8,8,4,3072]{3,1,0,2:T(8,128)(2,1)}, u32[]{:S(2)}, u32[]{:S(2)}) collective-permute-start(bf16[8,8,4,3072]{3,1,0,2:T(8,128)(2,1)S(1)} %slice.56), channel_id=1, source_target_pairs={{0,2},{2,4},{4,6},{6,8},{8,10},{10,12},{12,14},{14,16},{16,18},{18... | collective-permute-start | bytes 4718600 | tf_op jit(solution)/shard_map/ppermute | solution.py:14
  165.4 26.7 %copy-start.12 = (s32[64,64]{0,1:T(8,128)S(1)}, s32[64,64]{0,1:T(8,128)}, u32[]{:S(2)}) copy-start(s32[64,64]{0,1:T(8,128)} %copy-done.11) | copy-start | bytes 49156
  189.3 5.7 %copy-start.17 = (f32[128]{0:T(128)S(1)}, f32[128]{0:T(128)}, u32[]{:S(2)}) copy-start(f32[128]{0:T(128)} %get-tuple-element.14) | copy-start | bytes 1540
  189.3 5.7 %copy-start.18 = (f32[128]{0:T(128)S(1)}, f32[128]{0:T(128)}, u32[]{:S(2)}) copy-start(f32[128]{0:T(128)} %get-tuple-element.12) | copy-start | bytes 1540
  189.3 102.4 %collective-permute-start.3 = (bf16[16,8,4,3072]{3,1,0,2:T(8,128)(2,1)S(1)}, bf16[16,8,4,3072]{3,1,0,2:T(8,128)(2,1)}, u32[]{:S(2)}, u32[]{:S(2)}) collective-permute-start(bf16[16,8,4,3072]{3,1,0,2:T(8,128)(2,1)S(1)} %fusion.3), channel_id=1, source_target_pairs={{0,1},{1,0},{2,3},{3,2},{4,5},{5,4},{6,7},{7,6},{8,9},{9,8},{10,11... | collective-permute-start | bytes 9437192 | tf_op jit(solution)/shard_map/ppermute | solution.py:14
where the time goes:
time: 299 us; the launch traced here: 298 us
  blocking collectives  95.8 us (32%)
  waiting for transfers between devices  90.2 us (30%)
  other arithmetic  34.4 us (12%)
  matrix products  31.4 us (11%)
  local copies, waits for them, and re-layouts  29.4 us (10%)
  starting transfers between devices  8.67 us (3%)
  between operations  8.46 us (3%)
    psum x1, blocking collectives, local(): lax.psum((jnp.stack([dgain_q, dgain_k]), table_local), ('row', 'col'))  95.8 us
    ppermute x4, waiting for transfers between devices, shifted(): return lax.ppermute(value, axis, pairs)  90.2 us
    ppermute x4, starting transfers between devices, shifted(): return lax.ppermute(value, axis, pairs)  8.67 us
    unnamed x48, local copies, waits for them, and re-layouts  7.83 us
    another operation x5, local copies, waits for them, and re-layouts, local(): jnp.stack([output, d_query, d_key, d_value], axis=2)  6.26 us
  transfers between devices with their start and end apart: 4, of which 3 were waited for; matrix products, arithmetic and copies ran while one was open for 5% of the time, Pallas kernels for 0%

commit v1 on v0

--- a/solution.py
+++ b/solution.py
@@ -6,6 +6,9 @@
 
 EPSILON = 1e-06
 NEG_FILL = -1e30
+chunk_touch = lambda arr, net_axis, along_axis: lax.psum(
+    lax.psum(arr, axis_name=net_axis), along_axis
+)
 
 
 def shifted(value, axis, steps):
@@ -167,7 +170,7 @@
     attention = results[:, :, 0]
     d_qkv = results[:, :, 1:]
     table_local = jnp.einsum("hqk,qkc->hc", d_bias, one_hot, precision=lax.Precision.HIGHEST)
-    totals = lax.psum((jnp.stack([dgain_q, dgain_k]), table_local), ("row", "col"))
+    totals = chunk_touch((jnp.stack([dgain_q, dgain_k]), table_local), "col", "row")
     return (attention, d_qkv, totals[0], totals[1].reshape(head_count, span_count, span_count))
 
 

time: 299 us -> 329 us (1.10)
  blocking collectives: 95.8 us -> 125 us
    psum x1 -> x2, blocking collectives: 95.8 us -> 125 us  [the longest x1 63.2 us: lax.psum(lax.psum(arr, axis_name=net_axis), along_axis)]
  transfers between devices with their start and end apart: 4 -> 4, of which waited for: 3 -> 3; matrix products, arithmetic and copies ran while one was open for 5% -> 4% of each run, Pallas kernels for 0% -> 0%
where the time goes in v1:
time: 329 us; the launch traced here: 328 us
  blocking collectives  125 us (38%)
  waiting for transfers between devices  90.2 us (27%)
  other arithmetic  34.4 us (10%)
  matrix products  31.4 us (10%)
  local copies, waits for them, and re-layouts  29.4 us (9%)
  starting transfers between devices  8.67 us (3%)
  between operations  8.46 us (3%)
    ppermute x4, waiting for transfers between devices, shifted(): return lax.ppermute(value, axis, pairs)  90.2 us
    psum x1, blocking collectives, lax.psum(lax.psum(arr, axis_name=net_axis), along_axis)  63.2 us
    psum x1, blocking collectives, lax.psum(arr, axis_name=net_axis)  61.9 us
    ppermute x4, starting transfers between devices, shifted(): return lax.ppermute(value, axis, pairs)  8.67 us
    unnamed x48, local copies, waits for them, and re-layouts  7.83 us
  transfers between devices with their start and end apart: 4, of which 3 were waited for; matrix products, arithmetic and copies ran while one was open for 4% of the time, Pallas kernels for 0%

profile of v1, /device:TPU:0, one launch (start us, length us, event | category | flops | bytes accessed | tf_op | source)
XLA Modules:
  0.0 327.6 jit_solution(12330337860898563708)
XLA Ops:
  0.6 1.5 pad_maximum_fusion
  2.2 5.5 %collective-permute-start = (bf16[8,8,4,3072]{3,1,2,0:T(8,128)(2,1)S(1)}, bf16[8,8,4,3072]{3,1,2,0:T(8,128)(2,1)}, u32[]{:S(2)}, u32[]{:S(2)}) collective-permute-start(bf16[8,8,4,3072]{3,1,2,0:T(8,128)(2,1)S(1)} %pad_maximum_fusion), channel_id=1, source_target_pairs={{0,30},{2,0},{4,2},{6,4},{8,6},{10,8},{12,10},{14,12},{16,14},{18,... | collective-permute-start | bytes 4718600 | tf_op jit(solution)/shard_map/ppermute | solution.py:17
  7.7 0.6 fusion.39
  10.2 15.4 %collective-permute-done = bf16[8,8,4,3072]{3,1,2,0:T(8,128)(2,1)} collective-permute-done((bf16[8,8,4,3072]{3,1,2,0:T(8,128)(2,1)S(1)}, bf16[8,8,4,3072]{3,1,2,0:T(8,128)(2,1)}, u32[]{:S(2)}, u32[]{:S(2)}) %collective-permute-start) | collective-permute-done | bytes 1572896 | tf_op jit(solution)/shard_map/ppermute | solution.py:17
  25.6 2.9 fusion.5
  28.5 1.6 collective-permute-start.1
  32.5 0.1 fusion.34
  32.7 0.1 eq.45
  32.8 0.1 add_add_fusion
  32.9 0.6 copy-done.11
  33.5 0.9 iota_compare_fusion
  34.4 4.5 %fusion.20 = f32[24,64,64]{2,0,1:T(8,128)} fusion(pred[64,64,225]{2,0,1:T(32,128)(4,1)S(1)} %iota_compare_fusion, f32[24,225]{0,1:T(8,128)S(1)} %reshape.290), kind=kOutput, calls=%fused_computation.52 | convolution fusion | flops 265420800 | bytes 1336416 | tf_op jit(solution)/shard_map/hc,qkc->hqk/dot_general | solution.py:119
  38.9 2.3 copy.53
  41.8 0.6 broadcast_multiply_fusion.6
  42.4 0.7 broadcast_compare_fusion
  43.1 53.5 %collective-permute-done.1 = bf16[16,8,4,3072]{3,1,2,0:T(8,128)(2,1)} collective-permute-done((bf16[16,8,4,3072]{3,1,2,0:T(8,128)(2,1)S(1)}, bf16[16,8,4,3072]{3,1,2,0:T(8,128)(2,1)}, u32[]{:S(2)}, u32[]{:S(2)}) %collective-permute-start.1) | collective-permute-done | bytes 3145760 | tf_op jit(solution)/shard_map/ppermute | solution.py:17
  96.6 4.0 %fusion.7 = bf16[16,8,4,3072]{3,1,2,0:T(8,128)(2,1)S(1)} fusion(s32[]{:T(128)S(6)} %select_n.71, bf16[16,8,4,3072]{3,1,2,0:T(8,128)(2,1)S(1)} %fusion.5, bf16[16,8,4,3072]{3,1,2,0:T(8,128)(2,1)} %collective-permute-done.1), kind=kLoop, calls=%fused_computation.17 | loop fusion | flops 6291456 | bytes 9437188 | tf_op jit(solution)/shard_map/concatenate | solution.py:134
  100.6 0.9 copy.76
  101.5 0.9 convert_reduce_fusion
  102.4 2.4 fusion.38
  104.8 1.9 fusion.12
  107.0 4.2 %add_select_fusion = f32[2,24,64,64]{2,3,1,0:T(8,128)S(1)} fusion(f32[24,64,64]{1,2,0:T(8,128)} %copy.53, pred[2,64,64]{1,2,0:T(8,128)(4,1)} %broadcast_compare_fusion, f32[2,64,24,128]{3,2,1,0:T(8,128)} %bitcast.113, f32[128]{0:T(128)S(1)} %get-tuple-element.37, f32[2,64,24]{1,2,0:T(8,128)S(1)} %copy.47, f32[2,64,24]{1,2,0:T(8,128)S(1)} %copy.45, ...), kind=kOutput, calls=%fused_computation.44 | convolution fusion | flops 54067200 | bytes 4383744 | tf_op jit(solution)/shard_map/wqhd,wkhd->whqk/dot_general | solution.py:75
  111.2 1.6 fusion.40
  112.9 3.6 %fusion.19 = bf16[2,64,24,128]{3,1,2,0:T(8,128)(2,1)} fusion(bf16[2,64,24,128]{3,2,1,0:T(8,128)(2,1)} %bitcast.120, f32[2,24,64]{2,1,0:T(8,128)S(1)} %get-tuple-element.40, f32[2,24,64,64]{2,3,1,0:T(8,128)} %copy-done.2), kind=kOutput, calls=%fused_computation.51 | convolution fusion | flops 51317824 | bytes 2371584 | tf_op jit(solution)/shard_map/whqk,wqhd->wkhd/dot_general | solution.py:97
  116.5 3.6 %fusion.18 = bf16[2,64,24,128]{3,1,2,0:T(8,128)(2,1)} fusion(bf16[2,64,24,128]{3,2,1,0:T(8,128)(2,1)} %bitcast.122, f32[2,24,64]{2,1,0:T(8,128)S(1)} %get-tuple-element.40, f32[2,24,64,64]{2,3,1,0:T(8,128)} %copy-done.2), kind=kOutput, calls=%fused_computation.50 | convolution fusion | flops 51317824 | bytes 2371584 | tf_op jit(solution)/shard_map/whqk,wkhd->wqhd/dot_general | solution.py:84
  120.1 2.5 copy.56
  122.6 2.2 stack.22
  124.8 2.5 copy.69
  127.3 2.2 stack.25
  129.5 2.6 multiply_reduce_fusion.2
  132.1 1.4 fusion.29
  133.5 0.7 copy-done.4
  134.2 4.8 %multiply_reduce_fusion = (f32[128]{0:T(128)}, f32[2,64,24]{1,2,0:T(8,128)S(1)}, f32[2,64,24]{1,2,0:T(8,128)S(1)}, f32[2,24,128,64]{2,3,1,0:T(8,128)}) fusion(f32[2,64,24,128]{3,2,1,0:T(8,128)S(1)} %bitcast.111, f32[2,64,24]{1,2,0:T(8,128)S(1)} %copy.50, f32[2,64,24]{1,2,0:T(8,128)S(1)} %copy.48, f32[128]{0:T(128)S(1)} %copy-done.20, ...), kind=kOutput, calls=%fused_computation.36 | convolution fusion | flops 55437184 | bytes 5187072 | tf_op jit(solution)/shard_map/whqk,wqhd->wkhd/dot_general | solution.py:94
  139.0 5.3 %multiply_reduce_fusion.1 = (f32[128]{0:T(128)}, f32[2,64,24]{1,2,0:T(8,128)S(1)}, f32[2,64,24]{1,2,0:T(8,128)S(1)}, f32[2,24,128,64]{2,3,1,0:T(8,128)}) fusion(f32[2,64,24,128]{3,2,1,0:T(8,128)S(1)} %bitcast.115, f32[2,64,24]{1,2,0:T(8,128)S(1)} %copy.47, f32[2,64,24]{1,2,0:T(8,128)S(1)} %copy.45, f32[128]{0:T(128)S(1)} %copy-done.19, ...), kind=kOutput, calls=%fused_computation.37 | convolution fusion | flops 55437184 | bytes 5187072 | tf_op jit(solution)/shard_map/whqk,wkhd->wqhd/dot_general | solution.py:90
  144.3 0.6 broadcast_multiply_fusion.2
  144.9 0.6 broadcast_multiply_fusion.3
  145.5 0.6 broadcast_multiply_fusion.4
  146.2 0.1 copy.62
  146.2 0.8 copy.63
  147.1 1.4 copy.66
  148.5 1.4 copy.67
  149.9 1.6 multiply_bitcast_fusion
  151.5 0.9 copy.64
  152.4 0.5 copy-done.8
  152.9 0.2 multiply_bitcast_fusion.1
  153.2 0.9 copy.60
  154.1 5.1 %multiply_convert_fusion = (bf16[16,8,1,24,128]{4,3,1,2,0:T(8,128)(2,1)}, bf16[16,8,1,24,128]{4,3,1,2,0:T(8,128)(2,1)}) fusion(f32[16,8,1,24,128]{4,3,1,2,0:T(8,128)S(1)} %bitcast.108, f32[16,8,24]{2,1,0:T(8,128)S(1)} %bitcast.129, f32[16,8,24]{2,1,0:T(8,128)S(1)} %get-tuple-element.48, f32[16,8,24]{2,1,0:T(8,128)S(1)} %bitcast.128, ...), kind=kLoop, calls=%fused_computation.38 | loop fusion | flops 7077888 | bytes 6390784 | tf_op jit(solution)/shard_map/convert.8
  159.2 1.5 stack.24
  160.8 0.3 stack.23
  161.3 1.0 copy-done.5
  162.4 0.1 slice.56
  162.5 1.5 copy-done
  165.4 21.3 %collective-permute-done.2 = bf16[8,8,4,3072]{3,1,0,2:T(8,128)(2,1)} collective-permute-done((bf16[8,8,4,3072]{3,1,0,2:T(8,128)(2,1)S(1)}, bf16[8,8,4,3072]{3,1,0,2:T(8,128)(2,1)}, u32[]{:S(2)}, u32[]{:S(2)}) %collective-permute-start.2) | collective-permute-done | bytes 1572896 | tf_op jit(solution)/shard_map/ppermute | solution.py:17
  186.7 2.6 fusion.3
  189.3 1.6 collective-permute-start.3
  192.1 2.8 convolution_bitcast_fusion
  194.9 61.9 %all-reduce.1 = (f32[2,128]{1,0:T(2,128)S(1)}, f32[24,225]{1,0:T(8,128)S(1)}) all-reduce(f32[2,128]{1,0:T(2,128)S(1)} %pad_maximum_fusion.1, f32[24,225]{1,0:T(8,128)S(1)} %convolution_bitcast_fusion), channel_id=1, replica_groups=mesh['row'=16,'col'=2] {'col'}, use_global_device_ids=true, to_apply=%region_13.14 | all-reduce | flops 5656 | bytes 45248 | tf_op jit(solution)/shard_map/psum | solution.py:10
  256.8 0.1 reshape.285
  256.9 63.2 %all-reduce = (f32[2,128]{1,0:T(2,128)}, f32[24,15,15]{2,1,0:T(8,128)S(1)}) all-reduce(f32[2,128]{1,0:T(2,128)S(1)} %get-tuple-element.24, f32[24,15,15]{2,1,0:T(8,128)S(1)} %reshape.285), channel_id=1, replica_groups=mesh['row'=16,'col'=2] {'row'}, use_global_device_ids=true, to_apply=%region_14.15 | all-reduce | flops 5656 | bytes 45248 | tf_op jit(solution)/shard_map/psum | solution.py:9
  320.1 0.8 copy.72
  321.0 4.0 %fusion.6 = bf16[16,8,4,3072]{3,1,0,2:T(8,128)(2,1)S(1)} fusion(s32[]{:T(128)S(6)} %select_n.80, bf16[16,8,4,3072]{3,1,0,2:T(8,128)(2,1)} %collective-permute-done.3, bf16[16,8,4,3072]{3,1,0,2:T(8,128)(2,1)S(1)} %fusion.3), kind=kLoop, calls=%fused_computation.16 | loop fusion | flops 6291456 | bytes 9437188 | tf_op jit(solution)/shard_map/concatenate | solution.py:168
  325.0 0.9 slice_bitcast_fusion
  325.9 0.2 slice.58
  326.1 1.6 copy.71
  (57 shorter events, 0.7 us)
Async XLA Ops:
  0.6 7.1 %copy-start.16 = (s32[2]{0:T(128)S(1)}, s32[2]{0:T(128)}, u32[]{:S(2)}) copy-start(s32[2]{0:T(128)} %param.10) | copy-start | bytes 28
  2.2 23.4 %collective-permute-start = (bf16[8,8,4,3072]{3,1,2,0:T(8,128)(2,1)S(1)}, bf16[8,8,4,3072]{3,1,2,0:T(8,128)(2,1)}, u32[]{:S(2)}, u32[]{:S(2)}) collective-permute-start(bf16[8,8,4,3072]{3,1,2,0:T(8,128)(2,1)S(1)} %pad_maximum_fusion), channel_id=1, source_target_pairs={{0,30},{2,0},{4,2},{6,4},{8,6},{10,8},{12,10},{14,12},{16,14},{18,... | collective-permute-start | bytes 4718600 | tf_op jit(solution)/shard_map/ppermute | solution.py:17
  10.2 22.3 %copy-start.14 = (s32[256,16]{0,1:T(8,128)S(1)}, s32[256,16]{0,1:T(8,128)}, u32[]{:S(2)}) copy-start(s32[256,16]{0,1:T(8,128)} %param.11) | copy-start | bytes 49156
  10.2 22.5 %copy-start.13 = (f32[24,15,15]{0,2,1:T(8,128)S(1)}, f32[24,15,15]{0,2,1:T(8,128)}, u32[]{:S(2)}) copy-start(f32[24,15,15]{0,2,1:T(8,128)} %param.9) | copy-start | bytes 64804
  28.5 68.1 %collective-permute-start.1 = (bf16[16,8,4,3072]{3,1,2,0:T(8,128)(2,1)S(1)}, bf16[16,8,4,3072]{3,1,2,0:T(8,128)(2,1)}, u32[]{:S(2)}, u32[]{:S(2)}) collective-permute-start(bf16[16,8,4,3072]{3,1,2,0:T(8,128)(2,1)S(1)} %fusion.5), channel_id=1, source_target_pairs={{0,1},{1,0},{2,3},{3,2},{4,5},{5,4},{6,7},{7,6},{8,9},{9,8},{10,11... | collective-permute-start | bytes 9437192 | tf_op jit(solution)/shard_map/ppermute | solution.py:17
  32.9 0.6 copy-start.11
  38.9 2.9 copy-start.15
  111.2 1.7 copy-start.2
  129.5 2.6 copy-start.1
  132.1 1.4 copy-start.3
  132.1 2.2 copy-start.4
  132.1 2.1 copy-start.20
  134.2 4.8 %copy-start.19 = (f32[128]{0:T(128)S(1)}, f32[128]{0:T(128)}, u32[]{:S(2)}) copy-start(f32[128]{0:T(128)} %get-tuple-element.35) | copy-start | bytes 1540
  151.5 1.4 copy-start.8
  153.2 0.9 copy-start.9
  153.2 0.9 copy-start.10
  159.2 1.6 copy-start.7
  159.2 1.9 copy-start.6
  161.2 1.1 copy-start.5
  162.4 1.7 copy-start
  164.1 22.6 %collective-permute-start.2 = (bf16[8,8,4,3072]{3,1,0,2:T(8,128)(2,1)S(1)}, bf16[8,8,4,3072]{3,1,0,2:T(8,128)(2,1)}, u32[]{:S(2)}, u32[]{:S(2)}) collective-permute-start(bf16[8,8,4,3072]{3,1,0,2:T(8,128)(2,1)S(1)} %slice.56), channel_id=1, source_target_pairs={{0,2},{2,4},{4,6},{6,8},{8,10},{10,12},{12,14},{14,16},{16,18},{18... | collective-permute-start | bytes 4718600 | tf_op jit(solution)/shard_map/ppermute | solution.py:17
  165.4 26.7 %copy-start.17 = (f32[128]{0:T(128)S(1)}, f32[128]{0:T(128)}, u32[]{:S(2)}) copy-start(f32[128]{0:T(128)} %get-tuple-element.14) | copy-start | bytes 1540
  165.4 26.7 %copy-start.18 = (f32[128]{0:T(128)S(1)}, f32[128]{0:T(128)}, u32[]{:S(2)}) copy-start(f32[128]{0:T(128)} %get-tuple-element.12) | copy-start | bytes 1540
  165.4 26.7 %copy-start.12 = (s32[64,64]{0,1:T(8,128)S(1)}, s32[64,64]{0,1:T(8,128)}, u32[]{:S(2)}) copy-start(s32[64,64]{0,1:T(8,128)} %copy-done.11) | copy-start | bytes 49156
  189.3 131.7 %collective-permute-start.3 = (bf16[16,8,4,3072]{3,1,0,2:T(8,128)(2,1)S(1)}, bf16[16,8,4,3072]{3,1,0,2:T(8,128)(2,1)}, u32[]{:S(2)}, u32[]{:S(2)}) collective-permute-start(bf16[16,8,4,3072]{3,1,0,2:T(8,128)(2,1)S(1)} %fusion.3), channel_id=1, source_target_pairs={{0,1},{1,0},{2,3},{3,2},{4,5},{5,4},{6,7},{7,6},{8,9},{9,8},{10,11... | collective-permute-start | bytes 9437192 | tf_op jit(solution)/shard_map/ppermute | solution.py:17
